TPU v7x, 32 devices: a whole 2x2x4 slice. The times are simulated.
32 devices in a mesh: atlas: 4 (over y, x), row: 2 (over core), col: 4 (over z).
Axes of the slice: x: 2, y: 2, z: 4, core: 2. Of those that a mesh axis runs over, the one named last changes fastest.
Arguments:
- cells: bfloat16 [4, 64, 1024], P('atlas', None, 'row'), may hold values from -4 to 4
- support: bfloat16 [64, 16384], P(None, 'col'), may hold values from -4 to 4
Outputs:
- cell_dual: float32 [4, 1024], P('atlas', 'row')
- support_dual: float32 [4, 16384], P('atlas', 'col')
- new_support: float32 [64, 16384], P(None, 'col')
All inputs are finite; a program needn't handle non-finite values.
Results may differ from a plain program's by a relative error of at most 0.001.
Values sent between devices are 32-bit elements; how exact they have to be, the bound alone decides.
No kernel may reach another device: no remote copies, remote signals or barrier semaphores. Data moves between devices by JAX's collectives and lax.ppermute only.
A program may use at most 64 MiB of HBM per device.

v0:
```python
import jax
import jax.numpy as jnp
from jax import lax
from jax.sharding import PartitionSpec as P

ITERS = 2
blur = 0.1


def combined_all(value, axis, join):
    pieces = jax.tree.map(lambda part: lax.all_gather(part, axis), value)
    head = jax.tree.map(lambda part: part[0], pieces)
    tail = jax.tree.map(lambda part: part[1:], pieces)
    subtotal, _ = lax.scan(lambda subtotal, slab: (join(subtotal, slab), None), head, tail)
    return subtotal


def lse_pair(first, second):
    top_one, total_one = first
    top_two, total_two = second
    peak = jnp.maximum(top_one, top_two)
    return (peak, total_one * jnp.exp(top_one - peak) + total_two * jnp.exp(top_two - peak))


def shards(cells, support):
    points = cells[0]
    dims, rows = points.shape
    columns = support.shape[1]
    width_block = min(512, columns)
    count = columns // width_block
    points_wide = points.astype(jnp.float32)
    squares_x = jnp.sum(jnp.square(points_wide), axis=0)
    squares_y = jnp.sum(jnp.square(support.astype(jnp.float32)), axis=0)
    total_cells = rows * lax.axis_size("row")
    total_support = columns * lax.axis_size("col")
    atlases = lax.axis_size("atlas")

    def tile_cost(start):
        piece = lax.dynamic_slice_in_dim(support, start, width_block, 1)
        near = lax.dynamic_slice_in_dim(squares_y, start, width_block, 0)
        cross = lax.dot_general(
            points, piece, (((0,), (0,)), ((), ())), preferred_element_type=jnp.float32
        )
        return (squares_x[:, None] + near[None, :] - 2.0 * cross) / dims

    def row_step(dual_g):

        def row_visit(index, carry):
            top, total = carry
            start = index * width_block
            gpart = lax.dynamic_slice_in_dim(dual_g, start, width_block, 0)
            logits = (gpart[None, :] - tile_cost(start)) / blur
            peak = jnp.maximum(top, jnp.max(logits, axis=1))
            total = total * jnp.exp(top - peak) + jnp.sum(jnp.exp(logits - peak[:, None]), axis=1)
            return (peak, total)

        start_carry = (jnp.full((rows,), -jnp.inf, jnp.float32), jnp.zeros((rows,), jnp.float32))
        top, total = lax.fori_loop(0, count, row_visit, start_carry)
        top, total = combined_all((top, total), "col", lse_pair)
        return blur * jnp.log(1.0 / total_cells) - blur * (top + jnp.log(total))

    def column_step(dual_f):

        def column_visit(index, carry):
            top, total = carry
            start = index * width_block
            logits = (dual_f[:, None] - tile_cost(start)) / blur
            peak = jnp.max(logits, axis=0)
            mass = jnp.sum(jnp.exp(logits - peak[None, :]), axis=0)
            return (
                lax.dynamic_update_slice_in_dim(top, peak, start, 0),
                lax.dynamic_update_slice_in_dim(total, mass, start, 0),
            )

        start_carry = (jnp.zeros((columns,), jnp.float32), jnp.zeros((columns,), jnp.float32))
        top, total = lax.fori_loop(0, count, column_visit, start_carry)
        top, total = combined_all((top, total), "row", lse_pair)
        return blur * jnp.log(1.0 / total_support) - blur * (top + jnp.log(total))

    dual_g = jnp.zeros((columns,), jnp.float32)
    dual_f = jnp.zeros((rows,), jnp.float32)
    for step in range(ITERS):
        dual_f = row_step(dual_g)
        dual_g = column_step(dual_f)

    def positions_visit(index, summed):
        start = index * width_block
        gpart = lax.dynamic_slice_in_dim(dual_g, start, width_block, 0)
        plan = jnp.exp((dual_f[:, None] + gpart[None, :] - tile_cost(start)) / blur)
        moved = jnp.dot(points_wide, plan, precision=lax.Precision.HIGHEST) * total_support
        return lax.dynamic_update_slice_in_dim(summed, moved, start, 1)

    terms = lax.fori_loop(0, count, positions_visit, jnp.zeros((dims, columns), jnp.float32))
    summed = lax.psum(terms, ("atlas", "row"))
    updated = summed / atlases
    return (dual_f[None, :], dual_g[None, :], updated)


def solution(mesh):
    in_specs = (P("atlas", None, "row"), P(None, "col"))
    out_specs = (P("atlas", "row"), P("atlas", "col"), P(None, "col"))
    return jax.shard_map(shards, mesh=mesh, in_specs=in_specs, out_specs=out_specs, check_vma=False)
```

profile of v0, /device:TPU:0, one launch (start us, length us, event | category | flops | bytes accessed | tf_op | source)
XLA Modules:
  0.0 182.5 jit_solution(9270883459431666822)
XLA Ops:
  7.3 0.9 multiply_reduce_fusion.1
  8.2 1.2 multiply_reduce_fusion
  9.4 6.2 %while.114 = (s32[]{:T(128)}, f32[512]{0:T(512)S(1)}, f32[512]{0:T(512)S(1)}, f32[512]{0:T(512)S(1)}, f32[4096]{0:T(1024)S(1)}, /*index=5*/bf16[64,4096]{1,0:T(8...) while((s32[]{:T(128)}, f32[512]{0:T(512)S(1)}, ...), condition=%wide.region_5.0_spmd.clone, body=%wide.region_2.0_spmd.clone.sunk | while | flops 35916292 | bytes 2263222 | solution.py:58
  15.6 13.6 %all-gather.8 = f32[4,1,512]{2,1,0:T(1,128)S(1)} all-gather(f32[1,1,512]{2,1,0:T(1,128)S(1)} %bitcast.124), channel_id=2, replica_groups=mesh['atlas'=4,'row'=2,'col'=4] {'col'}, dimensions={0}, use_global_device_ids=true | all-gather | bytes 10240 | tf_op jit(solution)/shard_map/all_gather | solution.py:11
  29.3 0.6 copy-done.4
  29.9 11.9 %all-gather.9 = f32[4,1,512]{2,1,0:T(1,128)S(1)} all-gather(f32[1,1,512]{2,1,0:T(1,128)S(1)} %bitcast.134), channel_id=3, replica_groups=mesh['atlas'=4,'row'=2,'col'=4] {'col'}, dimensions={0}, use_global_device_ids=true | all-gather | bytes 10240 | tf_op jit(solution)/shard_map/all_gather | solution.py:11
  41.8 0.7 slice-done.3
  42.5 0.7 slice-done.2
  43.4 10.0 %while.110 = (s32[]{:T(128)}, f32[4096]{0:T(1024)S(1)}, f32[4096]{0:T(1024)S(1)}, f32[512]{0:T(512)S(1)}, f32[512]{0:T(512)S(1)}, /*index=5*/f32[4096]{0:T(1024)...) while((s32[]{:T(128)}, f32[4096]{0:T(1024)S(1)}, ...), condition=%wide.region_11.12_spmd, body=%wide.region_8.11_spmd.sunk | while | flops 35912708 | bytes 2252979 | solution.py:76
  43.5 0.5 fusion.78
  44.7 0.5 fusion.78
  46.0 0.5 fusion.78
  47.3 0.5 fusion.78
  48.5 0.5 fusion.78
  49.8 0.5 fusion.78
  51.0 0.5 fusion.78
  52.2 0.5 fusion.78
  53.4 1.8 all-gather.3
  55.2 1.8 all-gather.2
  57.0 6.8 %while.115 = (s32[]{:T(128)}, f32[512]{0:T(512)S(1)}, f32[512]{0:T(512)S(1)}, f32[4096]{0:T(1024)S(1)}, f32[512]{0:T(512)S(1)}, /*index=5*/f32[4096]{0:T(1024)S(...) while((s32[]{:T(128)}, f32[512]{0:T(512)S(1)}, ...), condition=%wide.region_15.16_spmd.clone, body=%wide.region_12.0_spmd.clone.sunk | while | flops 35916292 | bytes 2269378 | solution.py:58
  57.2 0.4 fusion.91
  58.1 0.5 fusion.91
  58.9 0.4 fusion.91
  60.6 0.4 fusion.91
  61.5 0.5 fusion.91
  63.9 11.9 %all-gather.10 = f32[4,1,512]{2,1,0:T(1,128)S(1)} all-gather(f32[1,1,512]{2,1,0:T(1,128)S(1)} %bitcast.123), channel_id=6, replica_groups=mesh['atlas'=4,'row'=2,'col'=4] {'col'}, dimensions={0}, use_global_device_ids=true | all-gather | bytes 10240 | tf_op jit(solution)/shard_map/all_gather | solution.py:11
  75.8 0.6 copy-done.3
  76.4 11.9 %all-gather.11 = f32[4,1,512]{2,1,0:T(1,128)S(1)} all-gather(f32[1,1,512]{2,1,0:T(1,128)S(1)} %bitcast.133), channel_id=7, replica_groups=mesh['atlas'=4,'row'=2,'col'=4] {'col'}, dimensions={0}, use_global_device_ids=true | all-gather | bytes 10240 | tf_op jit(solution)/shard_map/all_gather | solution.py:11
  88.3 0.6 copy-done.5
  88.9 0.7 slice-done.1
  89.6 0.7 slice-done.5
  90.3 0.7 slice-done.4
  91.2 10.0 %while.112 = (s32[]{:T(128)}, f32[4096]{0:T(1024)S(1)}, f32[4096]{0:T(1024)S(1)}, f32[512]{0:T(512)S(1)}, f32[512]{0:T(512)S(1)}, /*index=5*/f32[4096]{0:T(1024)...) while((s32[]{:T(128)}, f32[4096]{0:T(1024)S(1)}, ...), condition=%wide.region_21.22_spmd, body=%wide.region_18.0_spmd.sunk | while | flops 35912708 | bytes 2252979 | solution.py:76
  91.3 0.5 fusion.80
  92.6 0.5 fusion.80
  93.8 0.5 fusion.80
  95.1 0.5 fusion.80
  96.4 0.5 fusion.80
  97.6 0.5 fusion.80
  98.9 0.5 fusion.80
  100.1 0.5 fusion.80
  101.2 1.8 all-gather.7
  103.0 1.8 all-gather.6
  104.9 12.0 %while.113 = (s32[]{:T(128)}, f32[64,4096]{1,0:T(8,128)S(1)}, f32[512]{0:T(512)S(1)}, f32[4096]{0:T(1024)S(1)}, f32[512]{0:T(512)S(1)}, /*index=5*/f32[4096]{0:T...) while((s32[]{:T(128)}, f32[64,4096]{1,0:T(8,128)S(1)}, ...), condition=%wide.region_23.24_spmd, body=%wide.region_22.23_spmd.sunk | while | flops 236748800 | bytes 2506939 | solution.py:93
  105.1 0.5 fusion.85
  105.6 0.8 fusion.86
  106.6 0.5 fusion.85
  107.1 0.8 fusion.86
  108.1 0.5 fusion.85
  108.6 0.8 fusion.86
  109.6 0.5 fusion.85
  110.1 0.8 fusion.86
  111.1 0.5 fusion.85
  111.6 0.8 fusion.86
  112.6 0.5 fusion.85
  113.1 0.8 fusion.86
  114.1 0.5 fusion.85
  114.6 0.8 fusion.86
  115.6 0.5 fusion.85
  116.1 0.8 fusion.86
  116.9 0.6 copy-done.6
  117.9 0.7 multiply_subtract_fusion.1
  118.6 54.8 %all-reduce.2.cloned.1.call-done = f32[64,4096]{1,0:T(8,128)} async-done(((f32[64,4096]{1,0:T(8,128)}), f32[64,4096]{1,0:T(8,128)}) %all-reduce.2.cloned.1.call-update) | async-done | bytes 1048592 | tf_op jit(solution)/shard_map/psum | solution.py:94
  173.4 2.3 %broadcast_multiply_fusion = f32[64,4096]{1,0:T(8,128)} fusion(f32[64,4096]{1,0:T(8,128)} %all-reduce.2.cloned.1.call-done), kind=kLoop, calls=%fused_computation.61 | loop fusion | flops 262144 | bytes 2097152 | tf_op jit(solution)/shard_map/div | solution.py:95
  (232 shorter events, 25.1 us)
Async XLA Ops:
  7.2 2.2 %copy-start.1 = (bf16[64,4096]{1,0:T(8,128)(2,1)S(1)}, bf16[64,4096]{1,0:T(8,128)(2,1)}, u32[]{:S(2)}) copy-start(bf16[64,4096]{1,0:T(8,128)(2,1)} %param.17) | copy-start | bytes 1572868
  7.2 166.2 %all-reduce.2.cloned.1.call-start = ((), (), s32[]{:S(2)}) async-start(), calls=%async_computation | async-start | bytes 2097152 | tf_op jit(solution)/shard_map/psum | solution.py:94
  8.2 1.2 copy-start.2
  29.3 0.6 copy-start.4
  41.8 0.7 slice-start.3
  42.5 0.7 slice-start.2
  75.8 0.6 copy-start.3
  88.3 0.6 copy-start.5
  88.9 0.7 slice-start.1
  89.6 0.7 slice-start.5
  90.3 0.7 slice-start.4
  90.3 0.7 slice-start
  116.9 0.6 copy-start.6
  116.9 1.0 copy-start
Sparse Core Ops, SparseCore 0:
  118.0 55.2 all-reduce.1
where the time goes:
time: 183 us; the launch traced here: 182 us
  blocking collectives  56.7 us (31%)
  waiting for transfers between devices  54.8 us (30%)
  matrix products  25.1 us (14%)
  local copies, waits for them, and re-layouts  18.8 us (10%)
  between operations  14.2 us (8%)
  other arithmetic  12 us (7%)
    all_gather x8, blocking collectives, combined_all(): pieces = jax.tree.map(lambda part: lax.all_gather(part, axis), value)  56.7 us
    psum x1, waiting for transfers between devices, shards(): summed = lax.psum(terms, ('atlas', 'row'))  54.8 us
    dot_general x40, matrix products, tile_cost(): lax.dot_general(points, piece, (((0,), (0,)), ((), ())), preferred_elemen...  18.7 us
    dot_general x8, matrix products, positions_visit(): jnp.dot(points_wide, plan, precision=lax.Precision.HIGHEST) * total_support  6.37 us
    dynamic_update_slice x16, local copies, waits for them, and re-layouts, column_visit(): lax.dynamic_update_slice_in_dim(top, peak, start, 0)  4.3 us
    dynamic_update_slice x16, local copies, waits for them, and re-layouts, column_visit(): lax.dynamic_update_slice_in_dim(total, mass, start, 0)  3.85 us
  transfers between devices with their start and end apart: 1, of which 1 were waited for; matrix products, arithmetic and copies ran while one was open for 0% of the time, Pallas kernels for 0%

commit v1 on v0

--- a/solution.py
+++ b/solution.py
@@ -91,7 +91,7 @@
         return lax.dynamic_update_slice_in_dim(summed, moved, start, 1)
 
     terms = lax.fori_loop(0, count, positions_visit, jnp.zeros((dims, columns), jnp.float32))
-    summed = lax.psum(terms, ("atlas", "row"))
+    summed = lax.psum(lax.psum(terms, "atlas"), "row")
     updated = summed / atlases
     return (dual_f[None, :], dual_g[None, :], updated)
 

time: 183 us -> 200 us (1.093)
  waiting for transfers between devices: 54.8 us -> 72.3 us
    psum x1 -> x2, waiting for transfers between devices: 54.8 us -> 72.2 us  [shards(): summed = lax.psum(lax.psum(terms, 'atlas'), 'row')]
  transfers between devices with their start and end apart: 1 -> 2, of which waited for: 1 -> 2; matrix products, arithmetic and copies ran while one was open for 0% -> 0% of each run, Pallas kernels for 0% -> 0%
where the time goes in v1:
time: 200 us
  waiting for transfers between devices  72.3 us (36%)
  blocking collectives  56.7 us (28%)
  matrix products  25.1 us (13%)
  local copies, waits for them, and re-layouts  18.8 us (9%)
  between operations  14.2 us (7%)
  other arithmetic  12 us (6%)
    psum x2, waiting for transfers between devices, shards(): summed = lax.psum(lax.psum(terms, 'atlas'), 'row')  72.2 us
    all_gather x8, blocking collectives, combined_all(): pieces = jax.tree.map(lambda part: lax.all_gather(part, axis), value)  56.7 us
    dot_general x40, matrix products, tile_cost(): lax.dot_general(points, piece, (((0,), (0,)), ((), ())), preferred_elemen...  18.7 us
    dot_general x8, matrix products, positions_visit(): jnp.dot(points_wide, plan, precision=lax.Precision.HIGHEST) * total_support  6.37 us
    dynamic_update_slice x16, local copies, waits for them, and re-layouts, column_visit(): lax.dynamic_update_slice_in_dim(top, peak, start, 0)  4.3 us
  transfers between devices with their start and end apart: 2, of which 2 were waited for; matrix products, arithmetic and copies ran while one was open for 0% of the time, Pallas kernels for 0%

profile of v1, /device:TPU:0, one launch (start us, length us, event | category | flops | bytes accessed | tf_op | source)
XLA Modules:
  0.0 200.0 jit_solution(7314482372878963799)
XLA Ops:
  7.3 0.9 multiply_reduce_fusion.1
  8.2 1.2 multiply_reduce_fusion
  9.4 6.2 %while.114 = (s32[]{:T(128)}, f32[512]{0:T(512)S(1)}, f32[512]{0:T(512)S(1)}, f32[512]{0:T(512)S(1)}, f32[4096]{0:T(1024)S(1)}, /*index=5*/bf16[64,4096]{1,0:T(8...) while((s32[]{:T(128)}, f32[512]{0:T(512)S(1)}, ...), condition=%wide.region_5.0_spmd.clone, body=%wide.region_2.0_spmd.clone.sunk | while | flops 35916292 | bytes 2263222 | solution.py:58
  15.6 13.6 %all-gather.8 = f32[4,1,512]{2,1,0:T(1,128)S(1)} all-gather(f32[1,1,512]{2,1,0:T(1,128)S(1)} %bitcast.124), channel_id=2, replica_groups=mesh['atlas'=4,'row'=2,'col'=4] {'col'}, dimensions={0}, use_global_device_ids=true | all-gather | bytes 10240 | tf_op jit(solution)/shard_map/all_gather | solution.py:11
  29.3 0.6 copy-done.4
  29.9 11.9 %all-gather.9 = f32[4,1,512]{2,1,0:T(1,128)S(1)} all-gather(f32[1,1,512]{2,1,0:T(1,128)S(1)} %bitcast.134), channel_id=3, replica_groups=mesh['atlas'=4,'row'=2,'col'=4] {'col'}, dimensions={0}, use_global_device_ids=true | all-gather | bytes 10240 | tf_op jit(solution)/shard_map/all_gather | solution.py:11
  41.8 0.7 slice-done.3
  42.5 0.7 slice-done.2
  43.4 10.0 %while.110 = (s32[]{:T(128)}, f32[4096]{0:T(1024)S(1)}, f32[4096]{0:T(1024)S(1)}, f32[512]{0:T(512)S(1)}, f32[512]{0:T(512)S(1)}, /*index=5*/f32[4096]{0:T(1024)...) while((s32[]{:T(128)}, f32[4096]{0:T(1024)S(1)}, ...), condition=%wide.region_11.12_spmd, body=%wide.region_8.11_spmd.sunk | while | flops 35912708 | bytes 2252979 | solution.py:76
  43.5 0.5 fusion.78
  44.7 0.5 fusion.78
  46.0 0.5 fusion.78
  47.3 0.5 fusion.78
  48.5 0.5 fusion.78
  49.8 0.5 fusion.78
  51.0 0.5 fusion.78
  52.2 0.5 fusion.78
  53.4 1.8 all-gather.3
  55.2 1.8 all-gather.2
  57.0 6.8 %while.115 = (s32[]{:T(128)}, f32[512]{0:T(512)S(1)}, f32[512]{0:T(512)S(1)}, f32[4096]{0:T(1024)S(1)}, f32[512]{0:T(512)S(1)}, /*index=5*/f32[4096]{0:T(1024)S(...) while((s32[]{:T(128)}, f32[512]{0:T(512)S(1)}, ...), condition=%wide.region_15.16_spmd.clone, body=%wide.region_12.0_spmd.clone.sunk | while | flops 35916292 | bytes 2269378 | solution.py:58
  58.1 0.5 fusion.91
  58.9 0.4 fusion.91
  60.6 0.4 fusion.91
  61.5 0.5 fusion.91
  63.9 11.9 %all-gather.10 = f32[4,1,512]{2,1,0:T(1,128)S(1)} all-gather(f32[1,1,512]{2,1,0:T(1,128)S(1)} %bitcast.123), channel_id=6, replica_groups=mesh['atlas'=4,'row'=2,'col'=4] {'col'}, dimensions={0}, use_global_device_ids=true | all-gather | bytes 10240 | tf_op jit(solution)/shard_map/all_gather | solution.py:11
  75.8 0.6 copy-done.3
  76.4 11.9 %all-gather.11 = f32[4,1,512]{2,1,0:T(1,128)S(1)} all-gather(f32[1,1,512]{2,1,0:T(1,128)S(1)} %bitcast.133), channel_id=7, replica_groups=mesh['atlas'=4,'row'=2,'col'=4] {'col'}, dimensions={0}, use_global_device_ids=true | all-gather | bytes 10240 | tf_op jit(solution)/shard_map/all_gather | solution.py:11
  88.3 0.6 copy-done.5
  88.9 0.7 slice-done.1
  89.6 0.7 slice-done.5
  90.3 0.7 slice-done.4
  91.2 10.0 %while.112 = (s32[]{:T(128)}, f32[4096]{0:T(1024)S(1)}, f32[4096]{0:T(1024)S(1)}, f32[512]{0:T(512)S(1)}, f32[512]{0:T(512)S(1)}, /*index=5*/f32[4096]{0:T(1024)...) while((s32[]{:T(128)}, f32[4096]{0:T(1024)S(1)}, ...), condition=%wide.region_21.22_spmd, body=%wide.region_18.0_spmd.sunk | while | flops 35912708 | bytes 2252979 | solution.py:76
  91.3 0.5 fusion.80
  92.6 0.5 fusion.80
  93.8 0.5 fusion.80
  95.1 0.5 fusion.80
  96.4 0.5 fusion.80
  97.6 0.5 fusion.80
  98.9 0.5 fusion.80
  100.1 0.5 fusion.80
  101.2 1.8 all-gather.7
  103.0 1.8 all-gather.6
  104.9 12.0 %while.113 = (s32[]{:T(128)}, f32[64,4096]{1,0:T(8,128)S(1)}, f32[512]{0:T(512)S(1)}, f32[4096]{0:T(1024)S(1)}, f32[512]{0:T(512)S(1)}, /*index=5*/f32[4096]{0:T...) while((s32[]{:T(128)}, f32[64,4096]{1,0:T(8,128)S(1)}, ...), condition=%wide.region_23.24_spmd, body=%wide.region_22.23_spmd.sunk | while | flops 236748800 | bytes 2506939 | solution.py:93
  105.1 0.5 fusion.85
  105.6 0.8 fusion.86
  106.6 0.5 fusion.85
  107.1 0.8 fusion.86
  108.1 0.5 fusion.85
  108.6 0.8 fusion.86
  109.6 0.5 fusion.85
  110.1 0.8 fusion.86
  111.1 0.5 fusion.85
  111.6 0.8 fusion.86
  112.6 0.5 fusion.85
  113.1 0.8 fusion.86
  114.1 0.5 fusion.85
  114.6 0.8 fusion.86
  115.6 0.5 fusion.85
  116.1 0.8 fusion.86
  116.9 0.6 copy-done.6
  118.0 51.1 %all-reduce.3.cloned.1.call-done = f32[64,4096]{1,0:T(8,128)} async-done(((f32[64,4096]{1,0:T(8,128)}), f32[64,4096]{1,0:T(8,128)}) %all-reduce.3.cloned.1.call-update) | async-done | bytes 1048592 | tf_op jit(solution)/shard_map/psum | solution.py:94
  169.1 0.7 multiply_subtract_fusion.1
  169.8 21.1 %all-reduce.5.cloned.1.call-done = f32[64,4096]{1,0:T(8,128)} async-done(((f32[64,4096]{1,0:T(8,128)}), f32[64,4096]{1,0:T(8,128)}) %all-reduce.5.cloned.1.call-update) | async-done | bytes 1048592 | tf_op jit(solution)/shard_map/psum | solution.py:94
  190.9 2.3 %broadcast_multiply_fusion = f32[64,4096]{1,0:T(8,128)} fusion(f32[64,4096]{1,0:T(8,128)} %all-reduce.5.cloned.1.call-done), kind=kLoop, calls=%fused_computation.61 | loop fusion | flops 262144 | bytes 2097152 | tf_op jit(solution)/shard_map/div | solution.py:95
  (235 shorter events, 25.6 us)
Async XLA Ops:
  7.2 2.2 %copy-start.1 = (bf16[64,4096]{1,0:T(8,128)(2,1)S(1)}, bf16[64,4096]{1,0:T(8,128)(2,1)}, u32[]{:S(2)}) copy-start(bf16[64,4096]{1,0:T(8,128)(2,1)} %param.17) | copy-start | bytes 1572868
  7.2 161.9 %all-reduce.3.cloned.1.call-start = ((), (), s32[]{:S(2)}) async-start(), calls=%async_computation | async-start | bytes 2097152 | tf_op jit(solution)/shard_map/psum | solution.py:94
  8.2 1.2 copy-start.2
  29.3 0.6 copy-start.4
  41.8 0.7 slice-start.3
  42.5 0.7 slice-start.2
  75.8 0.6 copy-start.3
  88.3 0.6 copy-start.5
  88.9 0.7 slice-start.1
  89.6 0.7 slice-start.5
  90.3 0.7 slice-start.4
  90.3 0.7 slice-start
  116.9 0.6 copy-start.6
  116.9 1.0 copy-start
  117.9 73.0 %all-reduce.5.cloned.1.call-start = ((), (), s32[]{:S(2)}) async-start(), calls=%async_computation.1 | async-start | bytes 2097152 | tf_op jit(solution)/shard_map/psum | solution.py:94
Sparse Core Ops, SparseCore 0:
  118.0 51.0 all-reduce.2
  171.4 19.4 all-reduce.4
